TPU v7x, 32 devices: a whole 2x2x4 slice. The times are simulated.
32 devices in a mesh: groups: 2 (over y), tok: 16 (over z, x, core).
Axes of the slice: x: 2, y: 2, z: 4, core: 2. Of those that a mesh axis runs over, the one named last changes fastest.
Arguments:
- queries: bfloat16 [1024, 2048], P(('groups', 'tok')), parts along dimension 0, may hold values from -6 to 6
- new_kv: bfloat16 [3072, 4096], P(('groups', 'tok')), parts along dimension 0, may hold values from -6 to 6
- prev_kv: bfloat16 [2, 3072, 4096], P(None, ('groups', 'tok')), parts along dimension 1, may hold values from -6 to 6
- base_step: int32 [32], P(('groups', 'tok')), parts along dimension 0, may hold values from 0 to 1
- live_counts: int32 [32], P('groups'), parts along dimension 0, may hold values from 1 to 96
- sketch: float32 [4096, 32], replicated, may hold values from -0.09375 to 0.09375
- cache: bfloat16 [64, 1536, 128], P(('groups', 'tok')), parts along dimension 0, may hold values from -6 to 6, as said below
- w_out: bfloat16 [2048, 1536], replicated, may hold values from -0.125 to 0.125
Outputs:
- projected: bfloat16 [1024, 1536], P(('groups', 'tok')), parts along dimension 0
There are 2 independent parts, one for each index of `groups`. A program takes and returns all parts, laid end to end along the dimension named above; an argument that names none is the same for every part. Nothing has to cross between parts.
Inputs may be any that keep to these rules, and one draw needn't show every extreme that they name: cache slots i and j hold the same values when i // 2 == j // 2 and i % 2 == j % 2.
All inputs are finite; a program needn't handle non-finite values.
Results may differ from a plain program's by a relative error of at most 0.019.
Values may be sent and summed in bfloat16 or wider, within the bound.
No kernel may reach another device: no remote copies, remote signals or barrier semaphores. Data moves between devices by JAX's collectives and lax.ppermute only.
A program may use at most 128 MiB of HBM per device.

v0:
```python
import math
import jax
import jax.numpy as jnp
from jax import lax
from jax.sharding import PartitionSpec as P

HD = 64
SWEEPS = 2
highest = lax.Precision.HIGHEST


def orthonormal(block_cols):
    gram_matrix = jnp.dot(block_cols.T, block_cols, precision=highest)
    lower_factor = jnp.linalg.cholesky(gram_matrix)
    return jax.scipy.linalg.solve_triangular(lower_factor, block_cols.T, lower=True).T


def compress(delta_block, sketch):
    basis_cols = orthonormal(jnp.dot(delta_block, sketch, precision=highest))
    for sweep_index in range(SWEEPS):
        inner = jnp.dot(delta_block.T, basis_cols, precision=highest)
        basis_cols = orthonormal(jnp.dot(delta_block, inner, precision=highest))
    right_factor = jnp.dot(basis_cols.T, delta_block, precision=highest)
    return (basis_cols.astype(jnp.bfloat16), right_factor.astype(jnp.bfloat16))


def spread_heads(matrix, head_groups, groups_q, width):
    lead = matrix.shape[0]
    per_group = matrix.reshape(lead, head_groups, width).transpose(1, 0, 2)
    copies = jnp.broadcast_to(per_group[:, None], (head_groups, groups_q, lead, width))
    return copies.reshape(head_groups * groups_q, lead, width)


def attend_head(pieces, live_keys):
    q_head, keys_values = pieces
    key_part = keys_values[:, :HD]
    value_part = keys_values[:, HD:]
    query_count = q_head.shape[0]
    block_rows = math.gcd(query_count, 512)

    def one_block(query_block):
        scores = jnp.dot(query_block, key_part.T, preferred_element_type=jnp.float32) * HD ** (-0.5)
        scores = jnp.where(live_keys[None, :], scores, -1e30)
        row_max = jnp.max(scores, axis=-1, keepdims=True)
        exponent = jnp.exp(scores - row_max)
        weights = (exponent / jnp.sum(exponent, axis=-1, keepdims=True)).astype(jnp.bfloat16)
        return jnp.dot(weights, value_part, preferred_element_type=jnp.float32).astype(jnp.bfloat16)

    return lax.map(one_block, q_head.reshape(query_count // block_rows, block_rows, HD)).reshape(
        query_count, HD
    )


def per_device(queries, new_kv, prev_kv, base_step, live_counts, sketch, cache, w_out):
    shards = lax.axis_size("tok")
    tok_rows = new_kv.shape[0]
    query_rows = queries.shape[0]
    head_count = queries.shape[1] // HD
    groups_q = max(1, shards // head_count)
    per_dev = head_count * groups_q // shards
    head_groups = head_count // per_dev
    part_rows = query_rows // groups_q
    width = per_dev * 2 * HD
    key_count = shards * tok_rows
    query_count = shards * part_rows
    prior = prev_kv[0].astype(jnp.float32)
    prior = jnp.where(base_step[0] == 1, prev_kv[1].astype(jnp.float32), prior)
    delta = new_kv.astype(jnp.float32) - prior
    left_factor, right_factor = compress(delta, sketch)
    rank_cols = left_factor.shape[1]
    q_blocks = queries.reshape(groups_q, part_rows, head_groups, per_dev * HD)
    q_blocks = q_blocks.transpose(2, 0, 1, 3).reshape(shards, part_rows, per_dev * HD)
    w_blocks = spread_heads(right_factor, head_groups, groups_q, width)
    q_here = lax.all_to_all(q_blocks, "tok", split_axis=0, concat_axis=0, tiled=True)
    u_here = lax.all_gather(left_factor, "tok", axis=0, tiled=True).reshape(
        shards, tok_rows, rank_cols
    )
    w_here = lax.all_to_all(w_blocks, "tok", split_axis=0, concat_axis=0, tiled=True)
    lowrank = jnp.einsum("str,src->stc", u_here, w_here, preferred_element_type=jnp.float32).astype(
        jnp.bfloat16
    )
    lowrank = lowrank.reshape(key_count, per_dev, 2 * HD).transpose(1, 0, 2)
    keys_values = (cache.astype(jnp.float32) + lowrank.astype(jnp.float32)).astype(jnp.bfloat16)
    live_keys = (jnp.arange(tok_rows, dtype=jnp.int32)[None, :] < live_counts[:, None]).reshape(
        key_count
    )
    q_heads = q_here.reshape(query_count, per_dev, HD).transpose(1, 0, 2)
    attended = lax.map(lambda pieces: attend_head(pieces, live_keys), (q_heads, keys_values))
    attended = attended.transpose(1, 0, 2).reshape(shards, part_rows, per_dev * HD)
    returned = lax.all_to_all(attended, "tok", split_axis=0, concat_axis=0, tiled=True)
    returned = returned.reshape(head_groups, groups_q, part_rows, per_dev * HD)
    row_block = returned.transpose(1, 2, 0, 3).reshape(query_rows, head_count * HD)
    return jnp.dot(row_block, w_out, preferred_element_type=jnp.float32).astype(jnp.bfloat16)


def solution(mesh):
    return jax.shard_map(
        per_device,
        mesh=mesh,
        in_specs=(
            P(("groups", "tok"), None),
            P(("groups", "tok"), None),
            P(None, ("groups", "tok"), None),
            P(("groups", "tok")),
            P("groups"),
            P(),
            P(("groups", "tok"), None, None),
            P(),
        ),
        out_specs=P(("groups", "tok"), None),
        check_vma=False,
    )
```

profile of v0, /device:TPU:0, one launch (start us, length us, event | category | flops | bytes accessed | tf_op | source)
XLA Modules:
  0.0 94.7 jit_solution(8483638808945009714)
XLA Ops:
  0.0 0.0 copy-start
  0.0 1.0 %copy.33 = bf16[4,8,16,128]{3,2,1,0:T(8,128)(2,1)S(1)} copy(bf16[4,8,16,128]{3,1,2,0:T(8,128)(2,1)} %bitcast.116) | data formatting | bytes 262144
  1.0 0.7 copy.43
  1.7 7.4 %all-to-all-start = ((bf16[16,32,128]{2,1,0:T(8,128)(2,1)}), bf16[16,32,128]{2,1,0:T(8,128)(2,1)S(1)}, u32[]{:S(2)}, u32[]{:S(2)}) async-start(bf16[16,32,128]{2,1,0:T(8,128)(2,1)} %bitcast.103), calls=%async_computation | async-start | bytes 262144 | tf_op jit(solution)/shard_map/all_to_all | solution.py:74
  9.7 1.9 %bitcast_subtract_fusion = f32[96,4096]{1,0:T(8,128)S(1)} fusion(bf16[96,4096]{1,0:T(8,128)(2,1)} %param.14, bf16[2,96,4096]{2,1,0:T(8,128)(2,1)} %param.15, pred[]{:T(512)} %bitcast.3), kind=kLoop, calls=%fused_computation.21 | loop fusion | flops 1966080 | bytes 3932161 | tf_op jit(solution)/shard_map/sub | solution.py:68
  11.6 0.0 copy-done
  11.6 1.3 %fusion.37 = f32[96,32]{0,1:T(8,128)S(1)} fusion(f32[96,4096]{1,0:T(8,128)S(1)} %bitcast_subtract_fusion, f32[4096,32]{0,1:T(8,128)S(1)} %copy-done), kind=kOutput, calls=%fused_computation.61 | convolution fusion | flops 150994944 | bytes 2109440 | tf_op jit(solution)/shard_map/dot_general | solution.py:19
  13.0 0.1 fusion.38
  13.1 0.1 copy.24
  13.2 2.9 %cholesky.59 = f32[32,32]{1,0:T(8,128)S(1)} custom-call(f32[32,32]{1,0:T(8,128)S(1)} %fusion.31), custom_call_target="Cholesky" | custom-call | tf_op jit(solution)/shard_map/jit(cholesky)/cholesky | solution.py:14
  16.2 0.6 compare_reduce_fusion.2
  16.8 0.7 fusion.17
  17.5 2.4 %custom-call.7 = f32[1,32,32]{1,2,0:T(8,128)S(1)} custom-call(f32[1,32,32]{2,1,0:T(8,128)S(1)} %fusion.17), custom_call_target="InvertDiagBlocksLowerTriangular" | custom-call | tf_op jit(solution)/shard_map/jit(_solve_triangular)/triangular_solve | solution.py:15
  19.9 0.2 fusion.28
  20.1 1.0 %fusion.39 = f32[4096,32]{0,1:T(8,128)S(1)} fusion(f32[96,4096]{1,0:T(8,128)S(1)} %bitcast_subtract_fusion, f32[32,96]{1,0:T(8,128)S(1)} %fusion.28), kind=kOutput, calls=%fused_computation.63 | convolution fusion | flops 150994944 | bytes 2109440 | tf_op jit(solution)/shard_map/dot_general | solution.py:21
  21.2 1.3 %fusion.40 = f32[96,32]{0,1:T(8,128)S(1)} fusion(f32[96,4096]{1,0:T(8,128)S(1)} %bitcast_subtract_fusion, f32[4096,32]{0,1:T(8,128)S(1)} %fusion.39), kind=kOutput, calls=%fused_computation.64 | convolution fusion | flops 150994944 | bytes 2109440 | tf_op jit(solution)/shard_map/dot_general | solution.py:22
  22.5 0.1 fusion.41
  22.7 0.1 copy.25
  22.7 2.9 %cholesky.70 = f32[32,32]{1,0:T(8,128)S(1)} custom-call(f32[32,32]{1,0:T(8,128)S(1)} %fusion.27), custom_call_target="Cholesky" | custom-call | tf_op jit(solution)/shard_map/jit(cholesky)/cholesky | solution.py:14
  25.7 0.6 compare_reduce_fusion.1
  26.3 0.7 fusion.18
  27.0 2.4 %custom-call.8 = f32[1,32,32]{1,2,0:T(8,128)S(1)} custom-call(f32[1,32,32]{2,1,0:T(8,128)S(1)} %fusion.18), custom_call_target="InvertDiagBlocksLowerTriangular" | custom-call | tf_op jit(solution)/shard_map/jit(_solve_triangular)/triangular_solve | solution.py:15
  29.4 0.2 fusion.24
  29.7 1.0 %fusion.42 = f32[4096,32]{0,1:T(8,128)S(1)} fusion(f32[96,4096]{1,0:T(8,128)S(1)} %bitcast_subtract_fusion, f32[32,96]{1,0:T(8,128)S(1)} %fusion.24), kind=kOutput, calls=%fused_computation.66 | convolution fusion | flops 150994944 | bytes 2109440 | tf_op jit(solution)/shard_map/dot_general | solution.py:21
  30.7 1.3 %fusion.43 = f32[96,32]{0,1:T(8,128)S(1)} fusion(f32[96,4096]{1,0:T(8,128)S(1)} %bitcast_subtract_fusion, f32[4096,32]{0,1:T(8,128)S(1)} %fusion.42), kind=kOutput, calls=%fused_computation.67 | convolution fusion | flops 150994944 | bytes 2109440 | tf_op jit(solution)/shard_map/dot_general | solution.py:22
  32.0 0.1 fusion.44
  32.2 0.1 copy.26
  32.3 2.9 %cholesky.81 = f32[32,32]{1,0:T(8,128)S(1)} custom-call(f32[32,32]{1,0:T(8,128)S(1)} %fusion.23), custom_call_target="Cholesky" | custom-call | tf_op jit(solution)/shard_map/jit(cholesky)/cholesky | solution.py:14
  35.2 0.6 compare_reduce_fusion
  35.9 0.7 fusion.19
  36.5 2.4 %custom-call.9 = f32[1,32,32]{1,2,0:T(8,128)S(1)} custom-call(f32[1,32,32]{2,1,0:T(8,128)S(1)} %fusion.19), custom_call_target="InvertDiagBlocksLowerTriangular" | custom-call | tf_op jit(solution)/shard_map/jit(_solve_triangular)/triangular_solve | solution.py:15
  39.0 0.2 fusion.20
  39.2 0.9 convolution_convert_fusion
  40.1 0.7 copy.42
  40.8 0.0 all-to-all-done
  40.8 6.0 %all-to-all-start.1 = ((bf16[16,32,256]{2,1,0:T(8,128)(2,1)}), bf16[16,32,256]{2,1,0:T(8,128)(2,1)S(1)}, u32[]{:S(2)}, u32[]{:S(2)}) async-start(bf16[16,32,256]{2,1,0:T(8,128)(2,1)} %bitcast.102), calls=%async_computation.1 | async-start | bytes 524288 | tf_op jit(solution)/shard_map/all_to_all | solution.py:78
  46.8 22.3 %all-gather = bf16[16,96,32]{1,2,0:T(8,128)(2,1)S(1)} all-gather(bf16[1,96,32]{1,2,0:T(8,128)(2,1)S(1)} %convert_bitcast_fusion), channel_id=1, replica_groups=mesh['groups'=2,'tok'=16] {'tok'}, dimensions={0}, use_global_device_ids=true | all-gather | bytes 104448 | tf_op jit(solution)/shard_map/all_gather | solution.py:75
  69.2 0.1 reshape.49
  69.4 0.0 all-to-all-done.1
  69.4 1.6 %fusion.14 = f32[16,96,256]{2,1,0:T(8,128)} fusion(bf16[16,96,32]{1,2,0:T(8,128)(2,1)S(1)} %all-gather, bf16[16,32,256]{2,1,0:T(8,128)(2,1)S(1)} %all-to-all-done.1), kind=kOutput, calls=%fused_computation.23 | convolution fusion | flops 25952256 | bytes 1933312 | tf_op jit(solution)/shard_map/str,src->stc/dot_general | solution.py:79
  71.0 2.1 %reshape.55 = f32[1536,2,128]{2,1,0:T(2,128)S(1)} reshape(f32[16,96,256]{2,1,0:T(8,128)} %fusion.14) | data formatting | bytes 3145728 | tf_op jit(solution)/shard_map/convert_element_type | solution.py:83
  73.0 0.0 copy-start.1
  73.0 1.3 %fusion.13 = bf16[2,1536,128]{2,1,0:T(8,128)(2,1)S(1)} fusion(f32[1536,2,128]{2,1,0:T(2,128)S(1)} %reshape.55, bf16[2,1536,128]{2,1,0:T(8,128)(2,1)} %param.19), kind=kLoop, calls=%fused_computation.20 | loop fusion | flops 1179648 | bytes 3145728 | tf_op jit(solution)/shard_map/convert_element_type | solution.py:83
  74.3 0.0 copy-done.1
  74.3 4.9 %while.11 = (s32[]{:T(128)}, bf16[2,512,64]{1,2,0:T(8,128)(2,1)S(1)}, bf16[2,512,64]{2,1,0:T(8,128)(2,1)S(1)}, bf16[2,1536,128]{2,1,0:T(8,128)(2,1)S(1)}, s32[16]{0:T(128)S(1)}, /*index=5*/s32[]{:T(128)}) while((s32[]{:T(128)}, bf16[2,512,64]{1,2,0:T(8,128)(2,1)S(1)}, bf16[2,512,64]{2,1,0:T(8,128)(2,1)S(1)}, ...), condition=%wide.region_5.8_spmd.clone, body=%wide.region_2.7_spmd.clone.sunk | while | flops 207651328 | bytes 11223697 | solution.py:88
  74.4 0.1 iota_compare_fusion.4
  74.5 0.1 broadcast_in_dim.43
  74.5 0.7 fusion.71
  75.2 0.6 fusion.72
  75.8 1.0 %fusion.73 = bf16[2,512,64]{1,2,0:T(8,128)(2,1)S(1)} fusion(bf16[2,512,64]{1,2,0:T(8,128)(2,1)S(1)} %get-tuple-element.130, s32[]{:T(128)} %get-tuple-element.129, f32[512,1536]{1,0:T(8,128)S(1)} %get-tuple-element.121, f32[512]{0:T(512)S(1)} %fusion.72, f32[512]{0:T(512)S(1)} %get-tuple-element.122, ...), kind=kOutput, calls=%fused_computation.9.clone.1 | convolution fusion | flops 103055360 | bytes 3608580 | tf_op jit(solution)/shard_map/while/body/eval_jaxpr/while/body/eval_jaxpr/dot_general | solution.py:47
  76.8 0.1 iota_compare_fusion.4
  76.9 0.1 broadcast_in_dim.43
  77.0 0.7 fusion.71
  77.7 0.6 fusion.72
  78.3 1.0 %fusion.73 = bf16[2,512,64]{1,2,0:T(8,128)(2,1)S(1)} fusion(bf16[2,512,64]{1,2,0:T(8,128)(2,1)S(1)} %get-tuple-element.130, s32[]{:T(128)} %get-tuple-element.129, f32[512,1536]{1,0:T(8,128)S(1)} %get-tuple-element.121, f32[512]{0:T(512)S(1)} %fusion.72, f32[512]{0:T(512)S(1)} %get-tuple-element.122, ...), kind=kOutput, calls=%fused_computation.9.clone.1 | convolution fusion | flops 103055360 | bytes 3608580 | tf_op jit(solution)/shard_map/while/body/eval_jaxpr/while/body/eval_jaxpr/dot_general | solution.py:47
  79.3 0.2 copy.30
  79.4 0.1 reshape.52
  79.6 10.5 %all_to_all.15 = bf16[16,32,128]{2,1,0:T(8,128)(2,1)S(1)} all-to-all(bf16[16,32,128]{2,1,0:T(8,128)(2,1)S(1)} %reshape.52), channel_id=1, replica_groups=mesh['groups'=2,'tok'=16] {'tok'}, dimensions={0} | all-to-all | bytes 262144 | tf_op jit(solution)/shard_map/all_to_all | solution.py:90
  90.1 0.1 copy.31
  90.1 4.6 %convolution_convert_fusion.1 = bf16[32,1536]{1,0:T(8,128)(2,1)} fusion(bf16[2048,1536]{1,0:T(8,128)(2,1)} %param.20, bf16[4,8,16,128]{3,2,1,0:T(8,128)(2,1)S(1)} %bitcast.112), kind=kOutput, calls=%fused_computation.18 | convolution fusion | flops 201375744 | bytes 6520832 | tf_op jit(solution)/shard_map/dot_general | solution.py:93
  (11 shorter events, 0.2 us)
Async XLA Ops:
  0.0 11.6 %copy-start = (f32[4096,32]{0,1:T(8,128)S(1)}, f32[4096,32]{0,1:T(8,128)}, u32[]{:S(2)}) copy-start(f32[4096,32]{0,1:T(8,128)} %param.18) | copy-start | bytes 1572868
  1.7 39.1 %all-to-all-start = ((bf16[16,32,128]{2,1,0:T(8,128)(2,1)}), bf16[16,32,128]{2,1,0:T(8,128)(2,1)S(1)}, u32[]{:S(2)}, u32[]{:S(2)}) async-start(bf16[16,32,128]{2,1,0:T(8,128)(2,1)} %bitcast.103), calls=%async_computation | async-start | bytes 262144 | tf_op jit(solution)/shard_map/all_to_all | solution.py:74
  40.8 28.6 %all-to-all-start.1 = ((bf16[16,32,256]{2,1,0:T(8,128)(2,1)}), bf16[16,32,256]{2,1,0:T(8,128)(2,1)S(1)}, u32[]{:S(2)}, u32[]{:S(2)}) async-start(bf16[16,32,256]{2,1,0:T(8,128)(2,1)} %bitcast.102), calls=%async_computation.1 | async-start | bytes 524288 | tf_op jit(solution)/shard_map/all_to_all | solution.py:78
  73.0 1.3 %copy-start.1 = (s32[16]{0:T(128)S(1)}, s32[16]{0:T(128)}, u32[]{:S(2)}) copy-start(s32[16]{0:T(128)} %param.17) | copy-start | bytes 196
where the time goes:
time: 95.2 us; the launch traced here: 94.7 us
  blocking collectives  32.8 us (34%)
  other arithmetic  24.6 us (26%)
  matrix products  17.5 us (18%)
  starting transfers between devices  13.4 us (14%)
  local copies, waits for them, and re-layouts  5.45 us (6%)
    all_gather x1, blocking collectives, per_device(): lax.all_gather(left_factor, 'tok', axis=0, tiled=True)  22.3 us
    another operation x9, other arithmetic, orthonormal(): lower_factor = jnp.linalg.cholesky(gram_matrix)  10.8 us
    all_to_all x1, blocking collectives, per_device(): lax.all_to_all(attended, 'tok', split_axis=0, concat_axis=0, tiled=True)  10.5 us
    another operation x6, other arithmetic, orthonormal(): jax.scipy.linalg.solve_triangular(lower_factor, block_cols.T, lower=True)  9.26 us
    all_to_all x1, starting transfers between devices, per_device(): lax.all_to_all(q_blocks, 'tok', split_axis=0, concat_axis=0, tiled=True)  7.39 us
    all_to_all x1, starting transfers between devices, per_device(): lax.all_to_all(w_blocks, 'tok', split_axis=0, concat_axis=0, tiled=True)  6.01 us
    dot_general x1, matrix products, per_device(): jnp.dot(row_block, w_out, preferred_element_type=jnp.float32)  4.56 us
    dot_general x2, matrix products, compress(): basis_cols = orthonormal(jnp.dot(delta_block, inner, precision=highest))  2.69 us
  transfers between devices with their start and end apart: 2, of which 0 were waited for; matrix products, arithmetic and copies ran while one was open for 33% of the time, Pallas kernels for 0%

commit v1 on v0

--- a/solution.py
+++ b/solution.py
@@ -7,6 +7,28 @@
 HD = 64
 SWEEPS = 2
 highest = lax.Precision.HIGHEST
+
+
+def laid_out(blocks, dim):
+    lengths = list(blocks.shape[1:])
+    lengths[dim] *= blocks.shape[0]
+    return jnp.moveaxis(blocks, 0, dim).reshape(lengths)
+
+
+def ring_gather(x, axis, dim):
+    peers = lax.axis_size(axis)
+    pairs = [(i, (i + 1) % peers) for i in range(peers)]
+    back = [(b, a) for a, b in pairs]
+    lower, upper = ([], [])
+    for turn in range(peers - 1):
+        if turn % 2 == 0:
+            lower.append(lax.ppermute(lower[-1] if lower else x, axis, pairs))
+        else:
+            upper.append(lax.ppermute(upper[-1] if upper else x, axis, back))
+    parts = jnp.stack([*lower[::-1], x, *upper])
+    shift = lax.axis_index(axis) - len(lower)
+    parts = parts[(jnp.arange(peers) - shift) % peers]
+    return laid_out(parts, dim)
 
 
 def orthonormal(block_cols):
@@ -72,9 +94,7 @@
     q_blocks = q_blocks.transpose(2, 0, 1, 3).reshape(shards, part_rows, per_dev * HD)
     w_blocks = spread_heads(right_factor, head_groups, groups_q, width)
     q_here = lax.all_to_all(q_blocks, "tok", split_axis=0, concat_axis=0, tiled=True)
-    u_here = lax.all_gather(left_factor, "tok", axis=0, tiled=True).reshape(
-        shards, tok_rows, rank_cols
-    )
+    u_here = ring_gather(left_factor, "tok", 0).reshape(shards, tok_rows, rank_cols)
     w_here = lax.all_to_all(w_blocks, "tok", split_axis=0, concat_axis=0, tiled=True)
     lowrank = jnp.einsum("str,src->stc", u_here, w_here, preferred_element_type=jnp.float32).astype(
         jnp.bfloat16

time: 95.2 us -> 122 us (1.28)
  starting transfers between devices: 13.4 us -> 41 us
  blocking collectives: 32.8 us -> 10.7 us
  waiting for transfers between devices: 0.01 us -> 21.8 us
    ppermute x0 -> x15, starting transfers between devices: none -> 31.5 us  [the longest x7 30.9 us: ring_gather(): upper.append(lax.ppermute(upper[-1] if upper else x, axis, back))]
    all_gather x1 -> x0, blocking collectives: 22.3 us -> none  [per_device(): lax.all_gather(left_factor, 'tok', axis=0, tiled=True)]
    ppermute x0 -> x15, waiting for transfers between devices: none -> 12.8 us  [the longest x8 10.3 us: ring_gather(): lower.append(lax.ppermute(lower[-1] if lower else x, axis, pairs))]
    all_to_all x1, waiting for transfers between devices: 0.01 us -> 8.99 us  [per_device(): lax.all_to_all(w_blocks, 'tok', split_axis=0, concat_axis=0, tiled=True)]
    all_to_all x1, starting transfers between devices: 6.01 us -> 3.72 us  [per_device(): lax.all_to_all(w_blocks, 'tok', split_axis=0, concat_axis=0, tiled=True)]
    all_to_all x1, starting transfers between devices: 7.39 us -> 5.82 us  [per_device(): lax.all_to_all(q_blocks, 'tok', split_axis=0, concat_axis=0, tiled=True)]
  transfers between devices with their start and end apart: 2 -> 17, of which waited for: 0 -> 8; matrix products, arithmetic and copies ran while one was open for 33% -> 3% of each run, Pallas kernels for 0% -> 0%
where the time goes in v1:
time: 122 us
  starting transfers between devices  41 us (34%)
  other arithmetic  24.6 us (20%)
  waiting for transfers between devices  21.8 us (18%)
  matrix products  17.5 us (14%)
  blocking collectives  10.7 us (9%)
  local copies, waits for them, and re-layouts  5.19 us (4%)
    ppermute x7, starting transfers between devices, ring_gather(): upper.append(lax.ppermute(upper[-1] if upper else x, axis, back))  30.9 us
    another operation x9, other arithmetic, orthonormal(): lower_factor = jnp.linalg.cholesky(gram_matrix)  10.8 us
    all_to_all x1, blocking collectives, per_device(): lax.all_to_all(attended, 'tok', split_axis=0, concat_axis=0, tiled=True)  10.7 us
    ppermute x8, waiting for transfers between devices, ring_gather(): lower.append(lax.ppermute(lower[-1] if lower else x, axis, pairs))  10.3 us
    another operation x6, other arithmetic, orthonormal(): jax.scipy.linalg.solve_triangular(lower_factor, block_cols.T, lower=True)  9.26 us
    all_to_all x1, waiting for transfers between devices, per_device(): lax.all_to_all(w_blocks, 'tok', split_axis=0, concat_axis=0, tiled=True)  8.99 us
    all_to_all x1, starting transfers between devices, per_device(): lax.all_to_all(q_blocks, 'tok', split_axis=0, concat_axis=0, tiled=True)  5.82 us
    dot_general x1, matrix products, per_device(): jnp.dot(row_block, w_out, preferred_element_type=jnp.float32)  4.56 us
  transfers between devices with their start and end apart: 17, of which 8 were waited for; matrix products, arithmetic and copies ran while one was open for 3% of the time, Pallas kernels for 0%

profile of v1, /device:TPU:0, one launch (start us, length us, event | category | flops | bytes accessed | tf_op | source)
XLA Modules:
  0.0 121.9 jit_solution(6758067918221121726)
XLA Ops:
  0.7 1.9 %bitcast_subtract_fusion = f32[96,4096]{1,0:T(8,128)S(1)} fusion(bf16[96,4096]{1,0:T(8,128)(2,1)} %param.14, bf16[2,96,4096]{2,1,0:T(8,128)(2,1)} %param.15, pred[]{:T(512)} %bitcast.3), kind=kLoop, calls=%fused_computation.22 | loop fusion | flops 1966080 | bytes 3932161 | tf_op jit(solution)/shard_map/sub | solution.py:90
  2.6 1.3 %fusion.39 = f32[96,32]{0,1:T(8,128)S(1)} fusion(f32[96,4096]{1,0:T(8,128)S(1)} %bitcast_subtract_fusion, f32[4096,32]{0,1:T(8,128)S(1)} %copy-done), kind=kOutput, calls=%fused_computation.85 | convolution fusion | flops 150994944 | bytes 2109440 | tf_op jit(solution)/shard_map/dot_general | solution.py:41
  4.0 0.1 fusion.40
  4.2 2.9 %cholesky.59 = f32[32,32]{1,0:T(8,128)S(1)} custom-call(f32[32,32]{1,0:T(8,128)S(1)} %fusion.31), custom_call_target="Cholesky" | custom-call | tf_op jit(solution)/shard_map/jit(cholesky)/cholesky | solution.py:36
  7.2 0.6 compare_reduce_fusion.2
  7.8 0.7 fusion.17
  8.5 2.4 %custom-call.7 = f32[1,32,32]{1,2,0:T(8,128)S(1)} custom-call(f32[1,32,32]{2,1,0:T(8,128)S(1)} %fusion.17), custom_call_target="InvertDiagBlocksLowerTriangular" | custom-call | tf_op jit(solution)/shard_map/jit(_solve_triangular)/triangular_solve | solution.py:37
  10.9 0.2 fusion.28
  11.1 1.0 fusion.41
  12.1 1.3 %fusion.42 = f32[96,32]{0,1:T(8,128)S(1)} fusion(f32[96,4096]{1,0:T(8,128)S(1)} %bitcast_subtract_fusion, f32[4096,32]{0,1:T(8,128)S(1)} %fusion.41), kind=kOutput, calls=%fused_computation.88 | convolution fusion | flops 150994944 | bytes 2109440 | tf_op jit(solution)/shard_map/dot_general | solution.py:44
  13.5 0.1 fusion.43
  13.7 2.9 %cholesky.70 = f32[32,32]{1,0:T(8,128)S(1)} custom-call(f32[32,32]{1,0:T(8,128)S(1)} %fusion.27), custom_call_target="Cholesky" | custom-call | tf_op jit(solution)/shard_map/jit(cholesky)/cholesky | solution.py:36
  16.7 0.6 compare_reduce_fusion.1
  17.3 0.7 fusion.18
  18.0 2.4 %custom-call.8 = f32[1,32,32]{1,2,0:T(8,128)S(1)} custom-call(f32[1,32,32]{2,1,0:T(8,128)S(1)} %fusion.18), custom_call_target="InvertDiagBlocksLowerTriangular" | custom-call | tf_op jit(solution)/shard_map/jit(_solve_triangular)/triangular_solve | solution.py:37
  20.4 0.2 fusion.24
  20.7 1.0 fusion.44
  21.7 1.3 %fusion.45 = f32[96,32]{0,1:T(8,128)S(1)} fusion(f32[96,4096]{1,0:T(8,128)S(1)} %bitcast_subtract_fusion, f32[4096,32]{0,1:T(8,128)S(1)} %fusion.44), kind=kOutput, calls=%fused_computation.91 | convolution fusion | flops 150994944 | bytes 2109440 | tf_op jit(solution)/shard_map/dot_general | solution.py:44
  23.0 0.1 fusion.46
  23.3 2.9 %cholesky.81 = f32[32,32]{1,0:T(8,128)S(1)} custom-call(f32[32,32]{1,0:T(8,128)S(1)} %fusion.23), custom_call_target="Cholesky" | custom-call | tf_op jit(solution)/shard_map/jit(cholesky)/cholesky | solution.py:36
  26.2 0.6 compare_reduce_fusion
  26.9 0.7 fusion.19
  27.5 2.4 %custom-call.9 = f32[1,32,32]{1,2,0:T(8,128)S(1)} custom-call(f32[1,32,32]{2,1,0:T(8,128)S(1)} %fusion.19), custom_call_target="InvertDiagBlocksLowerTriangular" | custom-call | tf_op jit(solution)/shard_map/jit(_solve_triangular)/triangular_solve | solution.py:37
  30.0 0.2 fusion.20
  30.2 0.5 collective-permute-start
  30.8 6.3 %collective-permute-done = bf16[96,32]{0,1:T(8,128)(2,1)S(1)} collective-permute-done((bf16[96,32]{0,1:T(8,128)(2,1)S(1)}, bf16[96,32]{0,1:T(8,128)(2,1)S(1)}, u32[]{:S(2)}, u32[]{:S(2)}) %collective-permute-start) | collective-permute-done | bytes 6176 | tf_op jit(solution)/shard_map/ppermute | solution.py:25
  37.1 4.4 %collective-permute-start.8 = (bf16[96,32]{0,1:T(8,128)(2,1)S(1)}, bf16[96,32]{0,1:T(8,128)(2,1)S(1)}, u32[]{:S(2)}, u32[]{:S(2)}) collective-permute-start(bf16[96,32]{0,1:T(8,128)(2,1)S(1)} %convert_bitcast_fusion), channel_id=1, source_target_pairs={{1,0},{2,1},{3,2},{4,3},{5,4},{6,5},{7,6},{8,7},{9,8},{10,9},{11,1... | collective-permute-start | bytes 18440 | tf_op jit(solution)/shard_map/ppermute | solution.py:27
  41.5 1.4 %collective-permute-done.1 = bf16[96,32]{0,1:T(8,128)(2,1)S(1)} collective-permute-done((bf16[96,32]{0,1:T(8,128)(2,1)S(1)}, bf16[96,32]{0,1:T(8,128)(2,1)S(1)}, u32[]{:S(2)}, u32[]{:S(2)}) %collective-permute-start.1) | collective-permute-done | bytes 6176 | tf_op jit(solution)/shard_map/ppermute | solution.py:25
  42.9 4.4 %collective-permute-start.9 = (bf16[96,32]{0,1:T(8,128)(2,1)S(1)}, bf16[96,32]{0,1:T(8,128)(2,1)S(1)}, u32[]{:S(2)}, u32[]{:S(2)}) collective-permute-start(bf16[96,32]{0,1:T(8,128)(2,1)S(1)} %collective-permute-done.8), channel_id=1, source_target_pairs={{1,0},{2,1},{3,2},{4,3},{5,4},{6,5},{7,6},{8,7},{9,8},{10,9},{11,1... | collective-permute-start | bytes 18440 | tf_op jit(solution)/shard_map/ppermute | solution.py:27
  47.3 1.3 %collective-permute-done.2 = bf16[96,32]{0,1:T(8,128)(2,1)S(1)} collective-permute-done((bf16[96,32]{0,1:T(8,128)(2,1)S(1)}, bf16[96,32]{0,1:T(8,128)(2,1)S(1)}, u32[]{:S(2)}, u32[]{:S(2)}) %collective-permute-start.2) | collective-permute-done | bytes 6176 | tf_op jit(solution)/shard_map/ppermute | solution.py:25
  48.7 4.4 %collective-permute-start.10 = (bf16[96,32]{0,1:T(8,128)(2,1)S(1)}, bf16[96,32]{0,1:T(8,128)(2,1)S(1)}, u32[]{:S(2)}, u32[]{:S(2)}) collective-permute-start(bf16[96,32]{0,1:T(8,128)(2,1)S(1)} %collective-permute-done.9), channel_id=1, source_target_pairs={{1,0},{2,1},{3,2},{4,3},{5,4},{6,5},{7,6},{8,7},{9,8},{10,9},{11,1... | collective-permute-start | bytes 18440 | tf_op jit(solution)/shard_map/ppermute | solution.py:27
  53.1 1.3 %collective-permute-done.3 = bf16[96,32]{0,1:T(8,128)(2,1)S(1)} collective-permute-done((bf16[96,32]{0,1:T(8,128)(2,1)S(1)}, bf16[96,32]{0,1:T(8,128)(2,1)S(1)}, u32[]{:S(2)}, u32[]{:S(2)}) %collective-permute-start.3) | collective-permute-done | bytes 6176 | tf_op jit(solution)/shard_map/ppermute | solution.py:25
  54.4 0.7 copy.43
  55.1 5.8 %all-to-all-start = ((bf16[16,32,128]{2,1,0:T(8,128)(2,1)}), bf16[16,32,128]{2,1,0:T(8,128)(2,1)S(1)}, u32[]{:S(2)}, u32[]{:S(2)}) async-start(bf16[16,32,128]{2,1,0:T(8,128)(2,1)} %bitcast.136), calls=%async_computation | async-start | bytes 262144 | tf_op jit(solution)/shard_map/all_to_all | solution.py:96
  61.0 4.4 %collective-permute-start.11 = (bf16[96,32]{0,1:T(8,128)(2,1)S(1)}, bf16[96,32]{0,1:T(8,128)(2,1)S(1)}, u32[]{:S(2)}, u32[]{:S(2)}) collective-permute-start(bf16[96,32]{0,1:T(8,128)(2,1)S(1)} %collective-permute-done.10), channel_id=1, source_target_pairs={{1,0},{2,1},{3,2},{4,3},{5,4},{6,5},{7,6},{8,7},{9,8},{10,9},{11,1... | collective-permute-start | bytes 18440 | tf_op jit(solution)/shard_map/ppermute | solution.py:27
  65.4 0.9 convolution_convert_fusion
  66.3 0.5 collective-permute-done.11
  66.7 4.4 %collective-permute-start.12 = (bf16[96,32]{0,1:T(8,128)(2,1)S(1)}, bf16[96,32]{0,1:T(8,128)(2,1)S(1)}, u32[]{:S(2)}, u32[]{:S(2)}) collective-permute-start(bf16[96,32]{0,1:T(8,128)(2,1)S(1)} %collective-permute-done.11), channel_id=1, source_target_pairs={{1,0},{2,1},{3,2},{4,3},{5,4},{6,5},{7,6},{8,7},{9,8},{10,9},{11,1... | collective-permute-start | bytes 18440 | tf_op jit(solution)/shard_map/ppermute | solution.py:27
  71.2 1.3 %collective-permute-done.12 = bf16[96,32]{0,1:T(8,128)(2,1)S(1)} collective-permute-done((bf16[96,32]{0,1:T(8,128)(2,1)S(1)}, bf16[96,32]{0,1:T(8,128)(2,1)S(1)}, u32[]{:S(2)}, u32[]{:S(2)}) %collective-permute-start.12) | collective-permute-done | bytes 6176 | tf_op jit(solution)/shard_map/ppermute | solution.py:27
  72.5 4.4 %collective-permute-start.13 = (bf16[96,32]{0,1:T(8,128)(2,1)S(1)}, bf16[96,32]{0,1:T(8,128)(2,1)S(1)}, u32[]{:S(2)}, u32[]{:S(2)}) collective-permute-start(bf16[96,32]{0,1:T(8,128)(2,1)S(1)} %collective-permute-done.12), channel_id=1, source_target_pairs={{1,0},{2,1},{3,2},{4,3},{5,4},{6,5},{7,6},{8,7},{9,8},{10,9},{11,1... | collective-permute-start | bytes 18440 | tf_op jit(solution)/shard_map/ppermute | solution.py:27
  76.9 0.7 copy.42
  77.7 0.6 collective-permute-done.13
  78.3 4.4 %collective-permute-start.14 = (bf16[96,32]{0,1:T(8,128)(2,1)S(1)}, bf16[96,32]{0,1:T(8,128)(2,1)S(1)}, u32[]{:S(2)}, u32[]{:S(2)}) collective-permute-start(bf16[96,32]{0,1:T(8,128)(2,1)S(1)} %collective-permute-done.13), channel_id=1, source_target_pairs={{1,0},{2,1},{3,2},{4,3},{5,4},{6,5},{7,6},{8,7},{9,8},{10,9},{11,1... | collective-permute-start | bytes 18440 | tf_op jit(solution)/shard_map/ppermute | solution.py:27
  82.9 3.7 %all-to-all-start.1 = ((bf16[16,32,256]{2,1,0:T(8,128)(2,1)}), bf16[16,32,256]{2,1,0:T(8,128)(2,1)S(1)}, u32[]{:S(2)}, u32[]{:S(2)}) async-start(bf16[16,32,256]{2,1,0:T(8,128)(2,1)} %bitcast.135), calls=%async_computation.1 | async-start | bytes 524288 | tf_op jit(solution)/shard_map/all_to_all | solution.py:98
  86.6 0.6 gather_fusion
  87.2 0.1 reshape.95
  87.4 9.0 %all-to-all-done.1 = bf16[16,32,256]{2,1,0:T(8,128)(2,1)S(1)} async-done(((bf16[16,32,256]{2,1,0:T(8,128)(2,1)}), bf16[16,32,256]{2,1,0:T(8,128)(2,1)S(1)}, u32[]{:S(2)}, u32[]{:S(2)}) %all-to-all-start.1) | async-done | bytes 262176 | tf_op jit(solution)/shard_map/all_to_all | solution.py:98
  96.4 1.6 %fusion.14 = f32[16,96,256]{2,1,0:T(8,128)} fusion(bf16[16,96,32]{1,2,0:T(8,128)(2,1)S(1)} %gather_fusion, bf16[16,32,256]{2,1,0:T(8,128)(2,1)S(1)} %all-to-all-done.1), kind=kOutput, calls=%fused_computation.24 | convolution fusion | flops 25952256 | bytes 1933312 | tf_op jit(solution)/shard_map/str,src->stc/dot_general | solution.py:99
  97.9 2.1 %reshape.100 = f32[1536,2,128]{2,1,0:T(2,128)S(1)} reshape(f32[16,96,256]{2,1,0:T(8,128)} %fusion.14) | data formatting | bytes 3145728 | tf_op jit(solution)/shard_map/convert_element_type | solution.py:103
  100.0 1.3 %fusion.13 = bf16[2,1536,128]{2,1,0:T(8,128)(2,1)S(1)} fusion(f32[1536,2,128]{2,1,0:T(2,128)S(1)} %reshape.100, bf16[2,1536,128]{2,1,0:T(8,128)(2,1)} %param.19), kind=kLoop, calls=%fused_computation.21 | loop fusion | flops 1179648 | bytes 3145728 | tf_op jit(solution)/shard_map/convert_element_type | solution.py:103
  101.3 4.9 %while.11 = (s32[]{:T(128)}, bf16[2,512,64]{1,2,0:T(8,128)(2,1)S(1)}, bf16[2,512,64]{2,1,0:T(8,128)(2,1)S(1)}, bf16[2,1536,128]{2,1,0:T(8,128)(2,1)S(1)}, s32[16]{0:T(128)S(1)}, /*index=5*/s32[]{:T(128)}) while((s32[]{:T(128)}, bf16[2,512,64]{1,2,0:T(8,128)(2,1)S(1)}, bf16[2,512,64]{2,1,0:T(8,128)(2,1)S(1)}, ...), condition=%wide.region_5.8_spmd.clone, body=%wide.region_2.7_spmd.clone.sunk | while | flops 207651328 | bytes 11223697 | solution.py:108
  101.4 0.1 iota_compare_fusion.4
  101.5 0.1 broadcast_in_dim.44
  101.5 0.7 fusion.73
  102.2 0.6 fusion.74
  102.8 1.0 fusion.75
  103.9 0.1 broadcast_in_dim.44
  104.0 0.7 fusion.73
  104.7 0.6 fusion.74
  105.3 1.0 fusion.75
  106.3 0.2 copy.30
  106.4 0.1 reshape.97
  106.6 10.7 %all_to_all.15 = bf16[16,32,128]{2,1,0:T(8,128)(2,1)S(1)} all-to-all(bf16[16,32,128]{2,1,0:T(8,128)(2,1)S(1)} %reshape.97), channel_id=1, replica_groups=mesh['groups'=2,'tok'=16] {'tok'}, dimensions={0} | all-to-all | bytes 262144 | tf_op jit(solution)/shard_map/all_to_all | solution.py:110
  117.3 4.6 %convolution_convert_fusion.1 = bf16[32,1536]{1,0:T(8,128)(2,1)} fusion(bf16[2048,1536]{1,0:T(8,128)(2,1)} %param.20, bf16[4,8,16,128]{3,2,1,0:T(8,128)(2,1)S(1)} %bitcast.145), kind=kOutput, calls=%fused_computation.19 | convolution fusion | flops 201375744 | bytes 6520832 | tf_op jit(solution)/shard_map/dot_general | solution.py:113
  (57 shorter events, 0.8 us)
Async XLA Ops:
  0.0 2.6 %copy-start = (f32[4096,32]{0,1:T(8,128)S(1)}, f32[4096,32]{0,1:T(8,128)}, u32[]{:S(2)}) copy-start(f32[4096,32]{0,1:T(8,128)} %param.18) | copy-start | bytes 1572868
  21.7 32.7 %copy-start.1 = (bf16[32,2048]{1,0:T(8,128)(2,1)S(1)}, bf16[32,2048]{1,0:T(8,128)(2,1)}, u32[]{:S(2)}) copy-start(bf16[32,2048]{1,0:T(8,128)(2,1)} %param.13) | copy-start | bytes 393220
  30.2 6.8 %collective-permute-start = (bf16[96,32]{0,1:T(8,128)(2,1)S(1)}, bf16[96,32]{0,1:T(8,128)(2,1)S(1)}, u32[]{:S(2)}, u32[]{:S(2)}) collective-permute-start(bf16[96,32]{0,1:T(8,128)(2,1)S(1)} %convert_bitcast_fusion), channel_id=1, source_target_pairs={{0,1},{1,2},{2,3},{3,4},{4,5},{5,6},{6,7},{7,8},{8,9},{9,10},{10,1... | collective-permute-start | bytes 18440 | tf_op jit(solution)/shard_map/ppermute | solution.py:25
  37.1 5.8 %collective-permute-start.1 = (bf16[96,32]{0,1:T(8,128)(2,1)S(1)}, bf16[96,32]{0,1:T(8,128)(2,1)S(1)}, u32[]{:S(2)}, u32[]{:S(2)}) collective-permute-start(bf16[96,32]{0,1:T(8,128)(2,1)S(1)} %collective-permute-done), channel_id=1, source_target_pairs={{0,1},{1,2},{2,3},{3,4},{4,5},{5,6},{6,7},{7,8},{8,9},{9,10},{10,1... | collective-permute-start | bytes 18440 | tf_op jit(solution)/shard_map/ppermute | solution.py:25
  37.1 5.8 %collective-permute-start.8 = (bf16[96,32]{0,1:T(8,128)(2,1)S(1)}, bf16[96,32]{0,1:T(8,128)(2,1)S(1)}, u32[]{:S(2)}, u32[]{:S(2)}) collective-permute-start(bf16[96,32]{0,1:T(8,128)(2,1)S(1)} %convert_bitcast_fusion), channel_id=1, source_target_pairs={{1,0},{2,1},{3,2},{4,3},{5,4},{6,5},{7,6},{8,7},{9,8},{10,9},{11,1... | collective-permute-start | bytes 18440 | tf_op jit(solution)/shard_map/ppermute | solution.py:27
  42.9 5.8 %collective-permute-start.2 = (bf16[96,32]{0,1:T(8,128)(2,1)S(1)}, bf16[96,32]{0,1:T(8,128)(2,1)S(1)}, u32[]{:S(2)}, u32[]{:S(2)}) collective-permute-start(bf16[96,32]{0,1:T(8,128)(2,1)S(1)} %collective-permute-done.1), channel_id=1, source_target_pairs={{0,1},{1,2},{2,3},{3,4},{4,5},{5,6},{6,7},{7,8},{8,9},{9,10},{10,1... | collective-permute-start | bytes 18440 | tf_op jit(solution)/shard_map/ppermute | solution.py:25
  42.9 5.8 %collective-permute-start.9 = (bf16[96,32]{0,1:T(8,128)(2,1)S(1)}, bf16[96,32]{0,1:T(8,128)(2,1)S(1)}, u32[]{:S(2)}, u32[]{:S(2)}) collective-permute-start(bf16[96,32]{0,1:T(8,128)(2,1)S(1)} %collective-permute-done.8), channel_id=1, source_target_pairs={{1,0},{2,1},{3,2},{4,3},{5,4},{6,5},{7,6},{8,7},{9,8},{10,9},{11,1... | collective-permute-start | bytes 18440 | tf_op jit(solution)/shard_map/ppermute | solution.py:27
  48.6 5.8 %collective-permute-start.3 = (bf16[96,32]{0,1:T(8,128)(2,1)S(1)}, bf16[96,32]{0,1:T(8,128)(2,1)S(1)}, u32[]{:S(2)}, u32[]{:S(2)}) collective-permute-start(bf16[96,32]{0,1:T(8,128)(2,1)S(1)} %collective-permute-done.2), channel_id=1, source_target_pairs={{0,1},{1,2},{2,3},{3,4},{4,5},{5,6},{6,7},{7,8},{8,9},{9,10},{10,1... | collective-permute-start | bytes 18440 | tf_op jit(solution)/shard_map/ppermute | solution.py:25
  48.7 12.3 %collective-permute-start.10 = (bf16[96,32]{0,1:T(8,128)(2,1)S(1)}, bf16[96,32]{0,1:T(8,128)(2,1)S(1)}, u32[]{:S(2)}, u32[]{:S(2)}) collective-permute-start(bf16[96,32]{0,1:T(8,128)(2,1)S(1)} %collective-permute-done.9), channel_id=1, source_target_pairs={{1,0},{2,1},{3,2},{4,3},{5,4},{6,5},{7,6},{8,7},{9,8},{10,9},{11,1... | collective-permute-start | bytes 18440 | tf_op jit(solution)/shard_map/ppermute | solution.py:27
  54.4 11.0 %collective-permute-start.4 = (bf16[96,32]{0,1:T(8,128)(2,1)S(1)}, bf16[96,32]{0,1:T(8,128)(2,1)S(1)}, u32[]{:S(2)}, u32[]{:S(2)}) collective-permute-start(bf16[96,32]{0,1:T(8,128)(2,1)S(1)} %collective-permute-done.3), channel_id=1, source_target_pairs={{0,1},{1,2},{2,3},{3,4},{4,5},{5,6},{6,7},{7,8},{8,9},{9,10},{10,1... | collective-permute-start | bytes 18440 | tf_op jit(solution)/shard_map/ppermute | solution.py:25
  55.1 27.7 %all-to-all-start = ((bf16[16,32,128]{2,1,0:T(8,128)(2,1)}), bf16[16,32,128]{2,1,0:T(8,128)(2,1)S(1)}, u32[]{:S(2)}, u32[]{:S(2)}) async-start(bf16[16,32,128]{2,1,0:T(8,128)(2,1)} %bitcast.136), calls=%async_computation | async-start | bytes 262144 | tf_op jit(solution)/shard_map/all_to_all | solution.py:96
  61.0 5.8 %collective-permute-start.11 = (bf16[96,32]{0,1:T(8,128)(2,1)S(1)}, bf16[96,32]{0,1:T(8,128)(2,1)S(1)}, u32[]{:S(2)}, u32[]{:S(2)}) collective-permute-start(bf16[96,32]{0,1:T(8,128)(2,1)S(1)} %collective-permute-done.10), channel_id=1, source_target_pairs={{1,0},{2,1},{3,2},{4,3},{5,4},{6,5},{7,6},{8,7},{9,8},{10,9},{11,1... | collective-permute-start | bytes 18440 | tf_op jit(solution)/shard_map/ppermute | solution.py:27
  65.4 5.8 %collective-permute-start.5 = (bf16[96,32]{0,1:T(8,128)(2,1)S(1)}, bf16[96,32]{0,1:T(8,128)(2,1)S(1)}, u32[]{:S(2)}, u32[]{:S(2)}) collective-permute-start(bf16[96,32]{0,1:T(8,128)(2,1)S(1)} %collective-permute-done.4), channel_id=1, source_target_pairs={{0,1},{1,2},{2,3},{3,4},{4,5},{5,6},{6,7},{7,8},{8,9},{9,10},{10,1... | collective-permute-start | bytes 18440 | tf_op jit(solution)/shard_map/ppermute | solution.py:25
  66.7 5.8 %collective-permute-start.12 = (bf16[96,32]{0,1:T(8,128)(2,1)S(1)}, bf16[96,32]{0,1:T(8,128)(2,1)S(1)}, u32[]{:S(2)}, u32[]{:S(2)}) collective-permute-start(bf16[96,32]{0,1:T(8,128)(2,1)S(1)} %collective-permute-done.11), channel_id=1, source_target_pairs={{1,0},{2,1},{3,2},{4,3},{5,4},{6,5},{7,6},{8,7},{9,8},{10,9},{11,1... | collective-permute-start | bytes 18440 | tf_op jit(solution)/shard_map/ppermute | solution.py:27
  71.2 5.8 %collective-permute-start.6 = (bf16[96,32]{0,1:T(8,128)(2,1)S(1)}, bf16[96,32]{0,1:T(8,128)(2,1)S(1)}, u32[]{:S(2)}, u32[]{:S(2)}) collective-permute-start(bf16[96,32]{0,1:T(8,128)(2,1)S(1)} %collective-permute-done.5), channel_id=1, source_target_pairs={{0,1},{1,2},{2,3},{3,4},{4,5},{5,6},{6,7},{7,8},{8,9},{9,10},{10,1... | collective-permute-start | bytes 18440 | tf_op jit(solution)/shard_map/ppermute | solution.py:25
  72.5 5.8 %collective-permute-start.13 = (bf16[96,32]{0,1:T(8,128)(2,1)S(1)}, bf16[96,32]{0,1:T(8,128)(2,1)S(1)}, u32[]{:S(2)}, u32[]{:S(2)}) collective-permute-start(bf16[96,32]{0,1:T(8,128)(2,1)S(1)} %collective-permute-done.12), channel_id=1, source_target_pairs={{1,0},{2,1},{3,2},{4,3},{5,4},{6,5},{7,6},{8,7},{9,8},{10,9},{11,1... | collective-permute-start | bytes 18440 | tf_op jit(solution)/shard_map/ppermute | solution.py:27
  76.9 5.8 %collective-permute-start.7 = (bf16[96,32]{0,1:T(8,128)(2,1)S(1)}, bf16[96,32]{0,1:T(8,128)(2,1)S(1)}, u32[]{:S(2)}, u32[]{:S(2)}) collective-permute-start(bf16[96,32]{0,1:T(8,128)(2,1)S(1)} %collective-permute-done.6), channel_id=1, source_target_pairs={{0,1},{1,2},{2,3},{3,4},{4,5},{5,6},{6,7},{7,8},{8,9},{9,10},{10,1... | collective-permute-start | bytes 18440 | tf_op jit(solution)/shard_map/ppermute | solution.py:25
  78.3 8.3 %collective-permute-start.14 = (bf16[96,32]{0,1:T(8,128)(2,1)S(1)}, bf16[96,32]{0,1:T(8,128)(2,1)S(1)}, u32[]{:S(2)}, u32[]{:S(2)}) collective-permute-start(bf16[96,32]{0,1:T(8,128)(2,1)S(1)} %collective-permute-done.13), channel_id=1, source_target_pairs={{1,0},{2,1},{3,2},{4,3},{5,4},{6,5},{7,6},{8,7},{9,8},{10,9},{11,1... | collective-permute-start | bytes 18440 | tf_op jit(solution)/shard_map/ppermute | solution.py:27
  82.9 13.5 %all-to-all-start.1 = ((bf16[16,32,256]{2,1,0:T(8,128)(2,1)}), bf16[16,32,256]{2,1,0:T(8,128)(2,1)S(1)}, u32[]{:S(2)}, u32[]{:S(2)}) async-start(bf16[16,32,256]{2,1,0:T(8,128)(2,1)} %bitcast.135), calls=%async_computation.1 | async-start | bytes 524288 | tf_op jit(solution)/shard_map/all_to_all | solution.py:98
  100.0 1.3 %copy-start.2 = (s32[16]{0:T(128)S(1)}, s32[16]{0:T(128)}, u32[]{:S(2)}) copy-start(s32[16]{0:T(128)} %param.17) | copy-start | bytes 196
